TPU v7x, 512 devices: a whole 4x8x8 slice. The times are simulated.
512 devices in a mesh: rows: 64 (over z, y_hi, core), chan: 8 (over y_lo, x).
Axes of the slice: x: 4, y: 8 (y_hi: 4, y_lo: 2; y = y_hi * 2 + y_lo), z: 8, core: 2. Of those that a mesh axis runs over, the one named last changes fastest.
Arguments:
- pair: bfloat16 [512, 512, 128], P('rows', 'chan'), may hold values from -6 to 6
- block_mask: int32 [4, 4], replicated, may hold values from 0 to 1, as said below
- w_in: bfloat16 [128, 640], replicated, may hold values from -0.5 to 0.5
- w_out: bfloat16 [128, 128], replicated, may hold values from -0.5 to 0.5
Outputs:
- update: bfloat16 [512, 512, 128], P('rows', 'chan')
Inputs may be any that keep to these rules, and one draw needn't show every extreme that they name: Every diagonal entry of block_mask is 1; other entries are 0 or 1.
All inputs are finite; a program needn't handle non-finite values.
Results may differ from a plain program's by a relative error of at most 0.0078.
Values may be sent and summed in bfloat16 or wider, within the bound.
A program may use at most 64 MiB of HBM per device.

v0:
```python
import jax
import jax.numpy as jnp
from jax import lax
from jax.sharding import PartitionSpec as P

BLOCK = 128


def layer_norm(values):
    mean = jnp.mean(values, axis=-1, keepdims=True)
    centered = values - mean
    var = jnp.mean(centered * centered, axis=-1, keepdims=True)
    return centered / jnp.sqrt(var + 1e-05)


def channel_product(left, piece):
    return jnp.einsum("cik,cjk->cij", left, piece, preferred_element_type=jnp.float32)


def on_device(pair, block_mask, w_in, w_out):
    rows_dev, cols_dev, width = pair.shape
    n_blocks = block_mask.shape[0]
    row_start = lax.axis_index("rows") * rows_dev
    col_start = lax.axis_index("chan") * cols_dev
    row_ids = row_start + lax.broadcasted_iota(jnp.int32, (rows_dev, n_blocks), 0)
    col_ids = col_start + lax.broadcasted_iota(jnp.int32, (cols_dev, n_blocks), 0)
    rows_hot = (
        row_ids // BLOCK == lax.broadcasted_iota(jnp.int32, (rows_dev, n_blocks), 1)
    ).astype(jnp.float32)
    cols_hot = (
        col_ids // BLOCK == lax.broadcasted_iota(jnp.int32, (cols_dev, n_blocks), 1)
    ).astype(jnp.float32)
    mask_float = block_mask.astype(jnp.float32)
    local_mask = jnp.dot(jnp.dot(rows_hot, mask_float), cols_hot.T)[:, :, None]
    normed = layer_norm(pair.astype(jnp.float32)).astype(jnp.bfloat16)
    proj = jnp.dot(normed.reshape(-1, width), w_in, preferred_element_type=jnp.float32).reshape(
        rows_dev, cols_dev, 5 * width
    )
    left = (jax.nn.sigmoid(proj[..., :width]) * proj[..., width : 2 * width] * local_mask).astype(
        jnp.bfloat16
    )
    right = (
        jax.nn.sigmoid(proj[..., 2 * width : 3 * width])
        * proj[..., 3 * width : 4 * width]
        * local_mask
    ).astype(jnp.bfloat16)
    gate = jax.nn.sigmoid(proj[..., 4 * width :])
    left_t = jnp.transpose(left, (2, 0, 1))
    right_t = jnp.transpose(right, (2, 0, 1))
    left_ch, right_ch = (
        lax.all_to_all(left_t, "chan", split_axis=0, concat_axis=2, tiled=True),
        lax.all_to_all(right_t, "chan", split_axis=0, concat_axis=2, tiled=True),
    )
    prod_ch = channel_product(left_ch, lax.all_gather(right_ch, "rows", axis=1, tiled=True))
    prod_back = lax.all_to_all(prod_ch, "chan", split_axis=2, concat_axis=0, tiled=True)
    prod = jnp.transpose(prod_back, (1, 2, 0))
    normed_prod = layer_norm(prod).astype(jnp.bfloat16)
    mixed = jnp.dot(
        normed_prod.reshape(-1, width), w_out, preferred_element_type=jnp.float32
    ).reshape(rows_dev, cols_dev, width)
    return (gate * mixed).astype(jnp.bfloat16)


def solution(mesh):
    placed = (P("rows", "chan", None), P(), P(), P())
    return jax.shard_map(
        on_device, mesh=mesh, in_specs=placed, out_specs=P("rows", "chan", None), check_vma=False
    )
```

profile of v0, /device:TPU:1, one launch (start us, length us, event | category | flops | bytes accessed | tf_op | source)
XLA Modules:
  0.0 163.0 jit_solution(1687024607968159567)
XLA Ops:
  6.5 0.0 copy-start
  6.5 0.0 all-gather.2.cloned.1.call-start
  6.6 1.1 convert_reduce_fusion
  7.7 1.2 fusion.6
  8.9 0.0 copy-done
  8.9 1.3 fusion.22
  10.2 0.0 copy-start.1
  10.2 1.1 fusion.1
  11.3 0.2 fusion.28
  11.5 0.2 copy.23
  11.7 0.2 reshape.37
  11.9 11.1 %all_to_all.54 = bf16[8,2,4096]{2,1,0:T(2,128)(2,1)S(1)} all-to-all(bf16[8,2,4096]{2,1,0:T(2,128)(2,1)S(1)} %reshape.37), channel_id=1, replica_groups=mesh['rows'=64,'chan'=8] {'chan'}, dimensions={0} | all-to-all | bytes 262144 | tf_op jit(solution)/shard_map/all_to_all | solution.py:52
  23.0 0.2 reshape.38
  23.2 0.2 copy.24
  23.4 0.9 all_to_all.46
  24.3 0.0 all-gather.2.cloned.1.call-update
  24.3 0.0 copy-done.1
  24.3 0.2 copy.21
  24.5 0.2 reshape.35
  24.7 7.8 %all_to_all.55 = bf16[8,2,4096]{2,1,0:T(2,128)(2,1)S(1)} all-to-all(bf16[8,2,4096]{2,1,0:T(2,128)(2,1)S(1)} %reshape.35), channel_id=1, replica_groups=mesh['rows'=64,'chan'=8] {'chan'}, dimensions={0} | all-to-all | bytes 262144 | tf_op jit(solution)/shard_map/all_to_all | solution.py:51
  32.6 0.2 reshape.36
  32.8 0.2 copy.22
  33.0 0.2 all_to_all.42
  33.2 100.0 %all-gather.2.cloned.1.call-done = bf16[16,512,512]{2,1,0:T(8,128)(2,1)} async-done(((bf16[16,8,512]{2,1,0:T(8,128)(2,1)}), bf16[16,512,512]{2,1,0:T(8,128)(2,1)}) %all-gather.2.cloned.1.call-update) | async-done | bytes 8388624 | tf_op jit(solution)/shard_map/all_gather | solution.py:54
  133.2 5.6 %fusion.41 = f32[16,8,512]{2,1,0:T(8,128)S(1)} fusion(bf16[16,8,512]{2,1,0:T(8,128)(2,1)S(1)} %all_to_all.42, bf16[16,512,512]{2,1,0:T(8,128)(2,1)} %all-gather.2.cloned.1.call-done), kind=kOutput, calls=%fused_computation.65 | convolution fusion | flops 67108864 | bytes 8781824 | tf_op jit(solution)/shard_map/cik,cjk->cij/dot_general | solution.py:17
  138.8 0.8 copy.25
  139.6 0.7 reshape.39
  140.4 10.4 %all_to_all.56 = f32[8,1,8192]{2,1,0:T(1,128)S(1)} all-to-all(f32[8,1,8192]{2,1,0:T(1,128)S(1)} %reshape.39), channel_id=1, replica_groups=mesh['rows'=64,'chan'=8] {'chan'}, dimensions={0} | all-to-all | bytes 524288 | tf_op jit(solution)/shard_map/all_to_all | solution.py:55
  150.8 0.5 broadcast.132
  151.3 1.3 reduce
  152.6 0.7 reshape.40
  153.3 0.0 copy-start.2
  153.3 0.6 copy.26
  154.0 0.1 bitcast_reduce_fusion
  154.1 0.1 multiply_reduce_fusion
  154.3 0.1 divide_convert_fusion
  154.3 0.0 copy-done.2
  154.3 1.8 %fusion = bf16[8,64,128]{2,1,0:T(8,128)(2,1)} fusion(f32[8,64,640]{2,1,0:T(8,128)} %copy-done.1, bf16[8,64,128]{1,0,2:T(8,128)(2,1)S(1)} %divide_convert_fusion, bf16[128,128]{1,0:T(8,128)(2,1)S(1)} %copy-done.2), kind=kOutput, calls=%fused_computation.1 | convolution fusion | flops 17104896 | bytes 557056 | tf_op jit(solution)/shard_map/dot_general | solution.py:58
  (8 shorter events, 0.1 us)
Async XLA Ops:
  6.5 2.4 %copy-start = (bf16[128,640]{1,0:T(8,128)(2,1)S(1)}, bf16[128,640]{1,0:T(8,128)(2,1)}, u32[]{:S(2)}) copy-start(bf16[128,640]{1,0:T(8,128)(2,1)} %param.6) | copy-start | bytes 491524
  6.5 126.6 %all-gather.2.cloned.1.call-start = ((), (), s32[]{:S(2)}) async-start(), calls=%async_computation.3 | async-start | bytes 8519680 | tf_op jit(solution)/shard_map/all_gather | solution.py:54
  10.2 14.1 %copy-start.1 = (f32[8,64,640]{2,1,0:T(8,128)}, f32[8,64,640]{2,1,0:T(8,128)S(1)}, u32[]{:S(2)}) copy-start(f32[8,64,640]{2,1,0:T(8,128)S(1)} %fusion.22) | copy-start | bytes 3932164
  153.3 1.0 copy-start.2
Sparse Core Ops, SparseCore 0:
  24.4 108.6 all-gather.1
where the time goes:
time: 163 us
  waiting for transfers between devices  100 us (61%)
  blocking collectives  29.3 us (18%)
  between operations  13.6 us (8%)
  matrix products  9.88 us (6%)
  local copies, waits for them, and re-layouts  6.17 us (4%)
  other arithmetic  4.1 us (3%)
    all_gather x1, waiting for transfers between devices, on_device(): lax.all_gather(right_ch, 'rows', axis=1, tiled=True)  100 us
    all_to_all x1, blocking collectives, on_device(): lax.all_to_all(right_t, 'chan', split_axis=0, concat_axis=2, tiled=True)  11.1 us
    all_to_all x1, blocking collectives, on_device(): lax.all_to_all(prod_ch, 'chan', split_axis=2, concat_axis=0, tiled=True)  10.4 us
    all_to_all x1, blocking collectives, on_device(): lax.all_to_all(left_t, 'chan', split_axis=0, concat_axis=2, tiled=True)  7.82 us
    dot_general x1, matrix products, channel_product(): jnp.einsum('cik,cjk->cij', left, piece, preferred_element_type=jnp.float32)  5.63 us
  transfers between devices with their start and end apart: 1, of which 1 were waited for; matrix products, arithmetic and copies ran while one was open for 0% of the time, Pallas kernels for 0%

commit v1 on v0

v1 whole, which is shorter than its diff:
```python
import functools

import jax
import jax.numpy as jnp
from jax import lax
from jax.experimental import pallas as pl
from jax.experimental.pallas import tpu as pltpu
from jax.sharding import PartitionSpec as P

BLOCK = 128
EPS = 1e-05
MESH = pl.DeviceIdType.MESH
NT = (((1,), (1,)), ((), ()))


def wait_bytes(ref, sem):
    pltpu.make_async_copy(ref, ref, sem).wait()


def kernel(
    n_z, n_rs, n_q,
    mask_ref, pair_ref, w_in_ref, w_out_ref, out_ref,
    stage, send_l, send_r, l_in, r_all, l_mat, out_send, prod_in, gate,
    a2a_send, a2a_recv, ring_send, ring_recv, out_sems,
):
    n_i, n_k, width = pair_ref.shape
    half = width // 2
    n_plane = n_rs * n_q
    row_at = lax.axis_index("rows")
    q = lax.axis_index("chan")
    z = row_at // n_rs
    rs = row_at % n_rs
    me = rs * n_q + q
    up = {"rows": lax.rem(z + 1, n_z) * n_rs + rs, "chan": q}
    down = {"rows": lax.rem(z + n_z - 1, n_z) * n_rs + rs, "chan": q}

    def plane_device(index):
        return {"rows": z * n_rs + index // n_q, "chan": index % n_q}

    barrier = pltpu.get_barrier_semaphore()

    @pl.loop(1, n_plane)
    def _(step):
        pl.semaphore_signal(
            barrier, inc=1, device_id=plane_device(lax.rem(me + step, n_plane)), device_id_type=MESH
        )

    for neighbour in (up, down):
        pl.semaphore_signal(barrier, inc=1, device_id=neighbour, device_id_type=MESH)

    cells = pair_ref[...].astype(jnp.float32).reshape(n_i * n_k, width)
    mean = jnp.mean(cells, axis=-1, keepdims=True)
    centered = cells - mean
    var = jnp.mean(centered * centered, axis=-1, keepdims=True)
    normed = (centered / jnp.sqrt(var + EPS)).astype(jnp.bfloat16)
    zeros = jnp.zeros((n_k, width), jnp.bfloat16)
    diag = jnp.concatenate(
        [
            jnp.concatenate(pieces, axis=1)
            for i in range(n_i)
            for block in (normed[i * n_k : (i + 1) * n_k],)
            for pieces in ((block, zeros), (zeros, block))
        ],
        axis=0,
    )
    w_t = w_in_ref[:, : 4 * width].astype(jnp.float32).T.astype(jnp.bfloat16)
    w_lhs = jnp.concatenate(
        [
            jnp.concatenate(
                [w_t[p * width : p * width + half], w_t[p * width + half : (p + 1) * width]], axis=1
            )
            for p in range(4)
        ],
        axis=0,
    )
    proj = lax.dot_general(w_lhs, diag, NT, preferred_element_type=jnp.float32)
    cell_mask = mask_ref[(row_at * n_i) // BLOCK, (q * n_k) // BLOCK].astype(jnp.float32)
    for part, ref in ((2, send_r), (0, send_l)):
        gated = (
            jax.nn.sigmoid(proj[part * half : (part + 1) * half])
            * proj[(part + 1) * half : (part + 2) * half]
            * cell_mask
        )
        for i in range(n_i):
            stage[pl.ds(i, half, stride=n_i), :] = gated[:, i * 2 * n_k : (i + 1) * 2 * n_k]
        ref[...] = stage[...].astype(jnp.bfloat16).reshape(ref.shape)

    pl.semaphore_wait(barrier, n_plane + 1)

    def exchange(src, dst, which):
        @pl.loop(1, n_plane)
        def _(step):
            target = lax.rem(me + step, n_plane)
            pltpu.make_async_remote_copy(
                src_ref=src.at[target],
                dst_ref=dst,
                send_sem=a2a_send.at[which],
                recv_sem=a2a_recv.at[which],
                device_id=plane_device(target),
                device_id_type=MESH,
            ).start()

        pltpu.make_async_copy(src.at[me], dst, a2a_recv.at[which]).start()

    exchange(send_r, r_all.at[z, q, rs], 0)
    exchange(send_l, l_in.at[q, rs], 1)

    gate[...] = jax.nn.sigmoid(
        jnp.dot(normed, w_in_ref[:, 4 * width :], preferred_element_type=jnp.float32)
    )

    far = n_z // 2
    n_chunks = 2
    q_chunk = n_q // n_chunks

    def ring_copy(direction, step, chunk):
        block = lax.rem(z + (n_z - step if direction == 0 else step), n_z)
        ref = r_all.at[block, pl.ds(chunk * q_chunk, q_chunk)]
        return pltpu.make_async_remote_copy(
            src_ref=ref,
            dst_ref=ref,
            send_sem=ring_send.at[direction, step, chunk],
            recv_sem=ring_recv.at[direction, step, chunk],
            device_id=up if direction == 0 else down,
            device_id_type=MESH,
        )

    def ring_arrival(direction, step, chunk):
        block = lax.rem(z + (n_z - step if direction == 0 else step), n_z)
        ref = r_all.at[block, pl.ds(chunk * q_chunk, q_chunk)]
        return pltpu.make_async_remote_copy(
            src_ref=ref,
            dst_ref=ref,
            send_sem=ring_send.at[direction, step - 1, chunk],
            recv_sem=ring_recv.at[direction, step - 1, chunk],
            device_id=up if direction == 0 else down,
            device_id_type=MESH,
        )

    def carried(direction, step):
        if step + 1 < far:
            return range(n_chunks)
        return range(0, n_chunks // 2) if direction == 0 else range(n_chunks // 2, n_chunks)

    wait_bytes(r_all.at[z], a2a_recv.at[0])
    started = []
    for chunk in range(n_chunks):
        for direction in (0, 1):
            if chunk in carried(direction, 0):
                ring_copy(direction, 0, chunk).start()
                started.append((direction, 0, chunk))

    wait_bytes(l_in, a2a_recv.at[1])
    low = lax.broadcasted_iota(jnp.int32, (n_rs * n_i, 2 * n_k), 1) < n_k
    for k in range(n_q):
        block = l_in[k].reshape(n_rs * n_i, 2 * n_k).astype(jnp.float32)
        both = jnp.concatenate([jnp.where(low, block, 0.0), jnp.where(low, 0.0, block)], axis=0)
        l_mat[:, k * 2 * n_k : (k + 1) * 2 * n_k] = both.astype(jnp.bfloat16)

    def multiply(block, slot):
        right = jnp.concatenate(
            [r_all[block, k].reshape(n_rs * n_i, 2 * n_k) for k in range(n_q)], axis=1
        )
        prod = lax.dot_general(l_mat[...], right, NT, preferred_element_type=jnp.float32)
        rows = n_rs * n_i
        joined = jnp.concatenate([prod[:rows], prod[rows:]], axis=1).astype(jnp.bfloat16)
        out_send[slot] = joined.reshape(n_rs, n_i, 2 * n_k)

        @pl.loop(0, n_rs)
        def _(step):
            target = lax.rem(rs + step, n_rs)
            local = jnp.logical_and(target == rs, block == q)

            @pl.when(local)
            def _():
                pltpu.make_async_copy(
                    out_send.at[slot, target], prod_in.at[me], out_sems.at[1]
                ).start()

            @pl.when(jnp.logical_not(local))
            def _():
                pltpu.make_async_remote_copy(
                    src_ref=out_send.at[slot, target],
                    dst_ref=prod_in.at[me],
                    send_sem=out_sems.at[0],
                    recv_sem=out_sems.at[1],
                    device_id={"rows": z * n_rs + target, "chan": block},
                    device_id_type=MESH,
                ).start()

    multiply(z, 0)
    for step in range(1, far + 1):
        for chunk in range(n_chunks):
            for direction in (0, 1):
                if chunk in carried(direction, step - 1):
                    ring_arrival(direction, step, chunk).wait_recv()
                    if step < far and chunk in carried(direction, step):
                        ring_copy(direction, step, chunk).start()
                        started.append((direction, step, chunk))
        if step < far:
            multiply(lax.rem(z + n_z - step, n_z), 2 * step - 1)
            multiply(lax.rem(z + step, n_z), 2 * step)
        else:
            multiply(lax.rem(z + step, n_z), 2 * step - 1)

    w_halves = jnp.concatenate([w_out_ref[:half], w_out_ref[half:]], axis=1)
    wait_bytes(prod_in, out_sems.at[1])
    stage[...] = prod_in[...].astype(jnp.float32).reshape(n_plane * n_i, 2 * n_k)
    turned = []
    for i in range(n_i):
        values = stage[pl.ds(i, half, stride=n_i), :]
        total = jnp.sum(values, axis=0, keepdims=True)
        mean = (total + pltpu.roll(total, n_k, 1)) * (1.0 / width)
        centered = values - mean
        square = jnp.sum(centered * centered, axis=0, keepdims=True)
        var = (square + pltpu.roll(square, n_k, 1)) * (1.0 / width)
        turned.append((centered / jnp.sqrt(var + EPS)).T.astype(jnp.bfloat16))
    mixed = jnp.dot(
        jnp.concatenate(turned, axis=0), w_halves, preferred_element_type=jnp.float32
    )
    for i in range(n_i):
        at = i * 2 * n_k
        summed = mixed[at : at + n_k, :width] + mixed[at + n_k : at + 2 * n_k, width:]
        out_ref[i] = (gate[i * n_k : (i + 1) * n_k] * summed).astype(jnp.bfloat16)

    others = pl.ds(0, n_plane - 1)
    wait_bytes(send_r.at[others], a2a_send.at[0])
    wait_bytes(send_l.at[others], a2a_send.at[1])
    for key in started:
        ring_copy(*key).wait_send()

    wait_bytes(prod_in.at[others], out_sems.at[0])


def solution(mesh):
    n_rows, n_q = mesh.shape["rows"], mesh.shape["chan"]

    def on_device(pair, block_mask, w_in, w_out):
        n_i, n_k, width = pair.shape
        half = width // 2
        n_rs = half // n_q
        n_z = n_rows // n_rs
        n_plane = n_rs * n_q
        tile = (n_i, 2 * n_k)
        vmem = pl.BlockSpec(memory_space=pltpu.VMEM)
        return pl.pallas_call(
            functools.partial(kernel, n_z, n_rs, n_q),
            out_shape=jax.ShapeDtypeStruct((n_i, n_k, width), jnp.bfloat16),
            in_specs=[pl.BlockSpec(memory_space=pltpu.SMEM), vmem, vmem, vmem],
            out_specs=vmem,
            scratch_shapes=[
                pltpu.VMEM((n_plane * n_i, 2 * n_k), jnp.float32),
                pltpu.VMEM((n_plane, *tile), jnp.bfloat16),
                pltpu.VMEM((n_plane, *tile), jnp.bfloat16),
                pltpu.VMEM((n_q, n_rs, *tile), jnp.bfloat16),
                pltpu.VMEM((n_z, n_q, n_rs, *tile), jnp.bfloat16),
                pltpu.VMEM((2 * n_rs * n_i, n_q * 2 * n_k), jnp.bfloat16),
                pltpu.VMEM((n_z, n_rs, *tile), jnp.bfloat16),
                pltpu.VMEM((n_plane, *tile), jnp.bfloat16),
                pltpu.VMEM((n_i * n_k, width), jnp.float32),
                pltpu.SemaphoreType.DMA((2,)),
                pltpu.SemaphoreType.DMA((2,)),
                pltpu.SemaphoreType.DMA((2, n_z // 2, 2)),
                pltpu.SemaphoreType.DMA((2, n_z // 2, 2)),
                pltpu.SemaphoreType.DMA((2,)),
            ],
            compiler_params=pltpu.CompilerParams(collective_id=0, has_side_effects=True),
        )(block_mask, pair, w_in, w_out)

    placed = (P("rows", "chan", None), P(), P(), P())
    return jax.shard_map(
        on_device, mesh=mesh, in_specs=placed, out_specs=P("rows", "chan", None), check_vma=False
    )
```

time: 163 us -> 51 us (0.31)
  the two profiles are of different devices: /device:TPU:1 before, /device:TPU:9 now
where the time goes in v1:
time: 51 us; the launch traced here: 50.9 us
  Pallas kernels  49.3 us (97%)
  local copies, waits for them, and re-layouts  1.57 us (3%)
    pallas_call x1, Pallas kernels, on_device(): pl.pallas_call(functools.partial(kernel, n_z, n_rs, n_q), out_shape=jax.S...  49.3 us
    unnamed x1, local copies, waits for them, and re-layouts  1.57 us

profile of v1, /device:TPU:9, one launch (start us, length us, event | category | flops | bytes accessed | tf_op | source)
XLA Modules:
  0.0 50.9 jit_solution(1498066944769557871)
XLA Ops:
  0.0 49.3 %shard_map.46 = bf16[8,64,128]{2,1,0:T(8,128)(2,1)} custom-call(s32[4,4]{1,0:T(4,128)} %mask_ref.1, bf16[8,64,128]{2,1,0:T(8,128)(2,1)} %pair_ref.1, bf16[128,640]{1,0:T(8,128)(2,1)} %w_in_ref.1, bf16[128,128]{1,0:T(8,128)(2,1)} %w_out_ref.1), custom_call_target="tpu_custom_call" | custom-call | tf_op jit(solution)/shard_map/pallas_call | solution.py:246
  49.3 1.6 %copy.6 = bf16[8,64,128]{2,1,0:T(8,128)(2,1)} copy(bf16[8,64,128]{2,1,0:T(8,128)(2,1)} %shard_map.46) | data formatting | bytes 262144

commit v2 on v1

v2 whole, which is shorter than its diff:
```python
import functools

import jax
import jax.numpy as jnp
from jax import lax
from jax.experimental import pallas as pl
from jax.experimental.pallas import tpu as pltpu
from jax.sharding import PartitionSpec as P

BLOCK = 128
EPS = 1e-05
MESH = pl.DeviceIdType.MESH
NT = (((1,), (1,)), ((), ()))


def wait_bytes(ref, sem):
    pltpu.make_async_copy(ref, ref, sem).wait()


def kernel(
    n_z, n_rs, n_q,
    mask_hbm, pair_hbm, w_in_hbm, w_out_hbm, out_ref,
    mask_ref, pair_ref, w_in_ref, w_out_ref, load_sems, stage, send_l, send_r, l_in, r_all, l_mat, out_send, prod_in, gate,
    a2a_send, a2a_recv, ring_send, ring_recv, out_sems,
):
    loads = [
        pltpu.make_async_copy(src, dst, load_sems.at[at])
        for at, (src, dst) in enumerate(
            [(pair_hbm, pair_ref), (w_in_hbm, w_in_ref), (mask_hbm, mask_ref), (w_out_hbm, w_out_ref)]
        )
    ]
    for load in loads:
        load.start()
    n_i, n_k, width = pair_ref.shape
    half = width // 2
    n_plane = n_rs * n_q
    row_at = lax.axis_index("rows")
    q = lax.axis_index("chan")
    z = lax.div(row_at, n_rs)
    rs = lax.rem(row_at, n_rs)
    me = rs * n_q + q
    up = {"rows": lax.rem(z + 1, n_z) * n_rs + rs, "chan": q}
    down = {"rows": lax.rem(z + n_z - 1, n_z) * n_rs + rs, "chan": q}

    def plane_device(index):
        return {"rows": z * n_rs + lax.div(index, n_q), "chan": lax.rem(index, n_q)}

    barrier = pltpu.get_barrier_semaphore()

    @pl.loop(1, n_plane)
    def _(step):
        pl.semaphore_signal(
            barrier, inc=1, device_id=plane_device(lax.rem(me + step, n_plane)), device_id_type=MESH
        )

    for neighbour in (up, down):
        pl.semaphore_signal(barrier, inc=1, device_id=neighbour, device_id_type=MESH)

    loads[0].wait()
    cells = pair_ref[...].astype(jnp.float32).reshape(n_i * n_k, width)
    mean = jnp.mean(cells, axis=-1, keepdims=True)
    centered = cells - mean
    var = jnp.mean(centered * centered, axis=-1, keepdims=True)
    normed = (centered / jnp.sqrt(var + EPS)).astype(jnp.bfloat16)
    zeros = jnp.zeros((n_k, width), jnp.bfloat16)
    diag = jnp.concatenate(
        [
            jnp.concatenate(pieces, axis=1)
            for i in range(n_i)
            for block in (normed[i * n_k : (i + 1) * n_k],)
            for pieces in ((block, zeros), (zeros, block))
        ],
        axis=0,
    )
    loads[1].wait()
    w_t = w_in_ref[:, : 4 * width].astype(jnp.float32).T.astype(jnp.bfloat16)
    w_lhs = jnp.concatenate(
        [
            jnp.concatenate(
                [w_t[p * width : p * width + half], w_t[p * width + half : (p + 1) * width]], axis=1
            )
            for p in range(4)
        ],
        axis=0,
    )
    loads[2].wait()
    cell_mask = mask_ref[lax.div(row_at * n_i, BLOCK), lax.div(q * n_k, BLOCK)].astype(jnp.float32)

    def project(part, ref):
        proj = lax.dot_general(
            w_lhs[part * half : (part + 2) * half], diag, NT, preferred_element_type=jnp.float32
        )
        gated = jax.nn.sigmoid(proj[:half]) * proj[half:] * cell_mask
        for i in range(n_i):
            stage[pl.ds(i, half, stride=n_i), :] = gated[:, i * 2 * n_k : (i + 1) * 2 * n_k]
        ref[...] = stage[...].astype(jnp.bfloat16).reshape(ref.shape)

    project(2, send_r)
    pl.semaphore_wait(barrier, n_plane + 1)

    def exchange(src, dst, which):
        @pl.loop(0, n_plane - 1)
        def _(step):
            away = lax.div(step + 1, 2) * (2 * lax.rem(step, 2) - 1)
            target = lax.rem(me + n_plane // 2 + n_plane + away, n_plane)
            pltpu.make_async_remote_copy(
                src_ref=src.at[target],
                dst_ref=dst,
                send_sem=a2a_send.at[which],
                recv_sem=a2a_recv.at[which],
                device_id=plane_device(target),
                device_id_type=MESH,
            ).start()

        pltpu.make_async_copy(src.at[me], dst, a2a_recv.at[which]).start()

    exchange(send_r, r_all.at[z, q, rs], 0)
    project(0, send_l)
    exchange(send_l, l_in.at[q, rs], 1)

    gate[...] = jax.nn.sigmoid(
        jnp.dot(normed, w_in_ref[:, 4 * width :], preferred_element_type=jnp.float32)
    )

    far = n_z // 2
    n_chunks = 4
    q_chunk = n_q // n_chunks
    depth = q_chunk * 2 * n_k
    rows = n_rs * n_i

    def origin(direction, step):
        return lax.rem(z + (n_z - step if direction == 0 else step), n_z)

    def ring_copy(direction, step, chunk, block):
        ref = r_all.at[block, pl.ds(chunk * q_chunk, q_chunk)]
        return pltpu.make_async_remote_copy(
            src_ref=ref,
            dst_ref=ref,
            send_sem=ring_send.at[direction, step, chunk],
            recv_sem=ring_recv.at[direction, step, chunk],
            device_id=up if direction == 0 else down,
            device_id_type=MESH,
        )

    def carried(direction, step):
        if step + 1 < far:
            return range(n_chunks)
        return range(0, n_chunks // 2) if direction == 0 else range(n_chunks // 2, n_chunks)

    started = []

    def forward(direction, step, chunk):
        if step < far and chunk in carried(direction, step):
            copy = ring_copy(direction, step, chunk, origin(direction, step))
            copy.start()
            started.append(copy)

    def arrive(direction, step, chunk):
        ring_copy(direction, step - 1, chunk, origin(direction, step)).wait_recv()
        forward(direction, step, chunk)

    def product(block, chunk):
        right = jnp.concatenate(
            [r_all[block, chunk * q_chunk + k].reshape(rows, 2 * n_k) for k in range(q_chunk)], axis=1
        )
        return lax.dot_general(
            l_mat[:, chunk * depth : (chunk + 1) * depth], right, NT, preferred_element_type=jnp.float32
        )

    def emit(prod, block, slot):
        joined = jnp.concatenate([prod[:rows], prod[rows:]], axis=1).astype(jnp.bfloat16)
        out_send[slot] = joined.reshape(n_rs, n_i, 2 * n_k)

        @pl.loop(0, n_rs)
        def _(step):
            target = lax.rem(rs + n_rs // 2 + step, n_rs)
            local = jnp.logical_and(target == rs, block == q)

            @pl.when(local)
            def _():
                pltpu.make_async_copy(
                    out_send.at[slot, target], prod_in.at[me], out_sems.at[1]
                ).start()

            @pl.when(jnp.logical_not(local))
            def _():
                pltpu.make_async_remote_copy(
                    src_ref=out_send.at[slot, target],
                    dst_ref=prod_in.at[me],
                    send_sem=out_sems.at[0],
                    recv_sem=out_sems.at[1],
                    device_id={"rows": z * n_rs + target, "chan": block},
                    device_id_type=MESH,
                ).start()

    def multiply(direction, step):
        block = origin(direction, step)
        total = product(block, 0)
        for chunk in range(1, n_chunks):
            total = total + product(block, chunk)
        emit(total, block, 2 * step - direction)

    wait_bytes(r_all.at[z], a2a_recv.at[0])
    for chunk in range(n_chunks):
        for direction in (0, 1):
            forward(direction, 0, chunk)

    for step in range(1, far):
        for chunk in range(n_chunks):
            for direction in (0, 1):
                arrive(direction, step, chunk)
            if step > 1 and chunk in (0, n_chunks // 2):
                multiply(0 if chunk == 0 else 1, step - 1)
        if step == 1:
            wait_bytes(l_in, a2a_recv.at[1])
            low = lax.broadcasted_iota(jnp.int32, (rows, 2 * n_k), 1) < n_k
            for k in range(n_q):
                block = l_in[k].reshape(rows, 2 * n_k).astype(jnp.float32)
                both = jnp.concatenate(
                    [jnp.where(low, block, 0.0), jnp.where(low, 0.0, block)], axis=0
                )
                l_mat[:, k * 2 * n_k : (k + 1) * 2 * n_k] = both.astype(jnp.bfloat16)
            multiply(0, 0)

    last = origin(0, far)
    total = None
    pairs = zip(carried(0, far - 1), carried(1, far - 1), strict=True)
    for at, chunks in enumerate(pairs):
        for direction in (0, 1):
            arrive(direction, far, chunks[direction])
            part = product(last, chunks[direction])
            total = part if total is None else total + part
        if at == 0:
            multiply(0, far - 1)
            multiply(1, far - 1)
    emit(total, last, 2 * far - 1)

    loads[3].wait()
    w_halves = jnp.concatenate([w_out_ref[:half], w_out_ref[half:]], axis=1)
    wait_bytes(prod_in, out_sems.at[1])
    stage[...] = prod_in[...].astype(jnp.float32).reshape(n_plane * n_i, 2 * n_k)
    turned = []
    for i in range(n_i):
        values = stage[pl.ds(i, half, stride=n_i), :]
        total = jnp.sum(values, axis=0, keepdims=True)
        mean = (total + pltpu.roll(total, n_k, 1)) * (1.0 / width)
        centered = values - mean
        square = jnp.sum(centered * centered, axis=0, keepdims=True)
        var = (square + pltpu.roll(square, n_k, 1)) * (1.0 / width)
        turned.append((centered / jnp.sqrt(var + EPS)).T.astype(jnp.bfloat16))
    mixed = jnp.dot(
        jnp.concatenate(turned, axis=0), w_halves, preferred_element_type=jnp.float32
    )
    for i in range(n_i):
        at = i * 2 * n_k
        summed = mixed[at : at + n_k, :width] + mixed[at + n_k : at + 2 * n_k, width:]
        out_ref[i] = (gate[i * n_k : (i + 1) * n_k] * summed).astype(jnp.bfloat16)

    others = pl.ds(0, n_plane - 1)
    wait_bytes(send_r.at[others], a2a_send.at[0])
    wait_bytes(send_l.at[others], a2a_send.at[1])
    for copy in started:
        copy.wait_send()

    wait_bytes(prod_in.at[others], out_sems.at[0])


def solution(mesh):
    n_rows, n_q = mesh.shape["rows"], mesh.shape["chan"]

    def on_device(pair, block_mask, w_in, w_out):
        n_i, n_k, width = pair.shape
        half = width // 2
        n_rs = half // n_q
        n_z = n_rows // n_rs
        n_plane = n_rs * n_q
        tile = (n_i, 2 * n_k)
        hbm = pl.BlockSpec(memory_space=pltpu.HBM)
        return pl.pallas_call(
            functools.partial(kernel, n_z, n_rs, n_q),
            out_shape=jax.ShapeDtypeStruct((n_i, n_k, width), jnp.bfloat16),
            in_specs=[hbm] * 4,
            out_specs=pl.BlockSpec(memory_space=pltpu.VMEM),
            scratch_shapes=[
                pltpu.SMEM(block_mask.shape, block_mask.dtype),
                pltpu.VMEM(pair.shape, pair.dtype),
                pltpu.VMEM(w_in.shape, w_in.dtype),
                pltpu.VMEM(w_out.shape, w_out.dtype),
                pltpu.SemaphoreType.DMA((4,)),
                pltpu.VMEM((n_plane * n_i, 2 * n_k), jnp.float32),
                pltpu.VMEM((n_plane, *tile), jnp.bfloat16),
                pltpu.VMEM((n_plane, *tile), jnp.bfloat16),
                pltpu.VMEM((n_q, n_rs, *tile), jnp.bfloat16),
                pltpu.VMEM((n_z, n_q, n_rs, *tile), jnp.bfloat16),
                pltpu.VMEM((2 * n_rs * n_i, n_q * 2 * n_k), jnp.bfloat16),
                pltpu.VMEM((n_z, n_rs, *tile), jnp.bfloat16),
                pltpu.VMEM((n_plane, *tile), jnp.bfloat16),
                pltpu.VMEM((n_i * n_k, width), jnp.float32),
                pltpu.SemaphoreType.DMA((2,)),
                pltpu.SemaphoreType.DMA((2,)),
                pltpu.SemaphoreType.DMA((2, n_z // 2, 4)),
                pltpu.SemaphoreType.DMA((2, n_z // 2, 4)),
                pltpu.SemaphoreType.DMA((2,)),
            ],
            compiler_params=pltpu.CompilerParams(
                collective_id=0, has_side_effects=True, vmem_limit_bytes=16 * 2**20
            ),
        )(*(pltpu.with_memory_space_constraint(x, pltpu.HBM) for x in (block_mask, pair, w_in, w_out)))

    placed = (P("rows", "chan", None), P(), P(), P())
    return jax.shard_map(
        on_device, mesh=mesh, in_specs=placed, out_specs=P("rows", "chan", None), check_vma=False
    )
```

time: 51 us -> 46.7 us (0.916)
  Pallas kernels: 49.3 us -> 45.9 us
  local copies, waits for them, and re-layouts: 1.57 us -> 0.66 us
    pallas_call x1, Pallas kernels: 49.3 us -> 45.9 us  [on_device(): pl.pallas_call(functools.partial(kernel, n_z, n_rs, n_q), out_shape=jax.S...]
    unnamed x1, local copies, waits for them, and re-layouts: 1.57 us -> 0.66 us
where the time goes in v2:
time: 46.7 us; the launch traced here: 46.6 us
  Pallas kernels  45.9 us (98%)
  local copies, waits for them, and re-layouts  0.66 us (1%)
    pallas_call x1, Pallas kernels, on_device(): pl.pallas_call(functools.partial(kernel, n_z, n_rs, n_q), out_shape=jax.S...  45.9 us

profile of v2, /device:TPU:9, one launch (start us, length us, event | category | flops | bytes accessed | tf_op | source)
XLA Modules:
  0.0 46.6 jit_solution(3967612115531794715)
XLA Ops:
  0.0 45.9 %shard_map.46 = bf16[8,64,128]{2,1,0:T(8,128)(2,1)S(1)} custom-call(s32[4,4]{1,0:T(4,128)} %mask_hbm.1, bf16[8,64,128]{2,1,0:T(8,128)(2,1)} %pair_hbm.1, bf16[128,640]{1,0:T(8,128)(2,1)} %w_in_hbm.1, bf16[128,128]{1,0:T(8,128)(2,1)} %w_out_hbm.1), custom_call_target="tpu_custom_call" | custom-call | tf_op jit(solution)/shard_map/pallas_call | solution.py:279
  45.9 0.7 %copy.6 = bf16[8,64,128]{2,1,0:T(8,128)(2,1)} copy(bf16[8,64,128]{2,1,0:T(8,128)(2,1)S(1)} %shard_map.46) | data formatting | bytes 262144

commit v3 on v2

--- a/solution.py
+++ b/solution.py
@@ -9,6 +9,8 @@
 
 BLOCK = 128
 EPS = 1e-05
+CORES = 2
+UNROLL = 4
 MESH = pl.DeviceIdType.MESH
 NT = (((1,), (1,)), ((), ()))
 
@@ -22,6 +24,7 @@
     mask_hbm, pair_hbm, w_in_hbm, w_out_hbm, out_ref,
     mask_ref, pair_ref, w_in_ref, w_out_ref, load_sems, stage, send_l, send_r, l_in, r_all, l_mat, out_send, prod_in, gate,
     a2a_send, a2a_recv, ring_send, ring_recv, out_sems,
+    near_sem, far_sem,
 ):
     loads = [
         pltpu.make_async_copy(src, dst, load_sems.at[at])
@@ -45,16 +48,28 @@
     def plane_device(index):
         return {"rows": z * n_rs + lax.div(index, n_q), "chan": lax.rem(index, n_q)}
 
+    n_parts = r_all.shape[1]
+    group = lax.div(rs, CORES)
+    core = lax.rem(rs, CORES)
+    n_group = CORES * n_q
+    opposite = n_parts // 2
+    near_first = sorted(range(n_parts), key=lambda part: min(part, n_parts - part))
+    partner = {"rows": row_at + 1 - 2 * core, "chan": q}
     barrier = pltpu.get_barrier_semaphore()
 
-    @pl.loop(1, n_plane)
-    def _(step):
-        pl.semaphore_signal(
-            barrier, inc=1, device_id=plane_device(lax.rem(me + step, n_plane)), device_id_type=MESH
-        )
-
+    def hello(device):
+        pl.semaphore_signal(barrier, inc=1, device_id=device, device_id_type=MESH)
+
+    for part in near_first[::-1]:
+        first = z * n_rs + lax.rem(group + part, n_parts) * CORES + (1 if part == opposite else 0)
+
+        @pl.loop(1 if part == 0 else 0, n_q, unroll=True)
+        def _(step):
+            hello({"rows": first, "chan": lax.rem(q + step, n_q)})
+
+    hello(partner)
     for neighbour in (up, down):
-        pl.semaphore_signal(barrier, inc=1, device_id=neighbour, device_id_type=MESH)
+        hello({"rows": neighbour["rows"] - core, "chan": q})
 
     loads[0].wait()
     cells = pair_ref[...].astype(jnp.float32).reshape(n_i * n_k, width)
@@ -96,43 +111,78 @@
         ref[...] = stage[...].astype(jnp.bfloat16).reshape(ref.shape)
 
     project(2, send_r)
-    pl.semaphore_wait(barrier, n_plane + 1)
-
-    def exchange(src, dst, which):
-        @pl.loop(0, n_plane - 1)
+
+    def tell(sem):
+        pl.semaphore_signal(sem, inc=1, device_id=partner, device_id_type=MESH)
+
+    def send(src, target, dst, send_sem, recv_sem):
+        pltpu.make_async_remote_copy(
+            src_ref=src.at[target],
+            dst_ref=dst,
+            send_sem=send_sem,
+            recv_sem=recv_sem,
+            device_id=plane_device(target),
+            device_id_type=MESH,
+        ).start()
+
+    r_slot = r_all.at[z, group, core, q]
+
+    def send_group(part):
+        target_group = lax.rem(group + part, n_parts)
+
+        @pl.loop(1 if part == 0 else 0, n_group, unroll=UNROLL)
         def _(step):
-            away = lax.div(step + 1, 2) * (2 * lax.rem(step, 2) - 1)
-            target = lax.rem(me + n_plane // 2 + n_plane + away, n_plane)
+            to = lax.rem(core * n_q + q + step, n_group)
             pltpu.make_async_remote_copy(
-                src_ref=src.at[target],
-                dst_ref=dst,
-                send_sem=a2a_send.at[which],
-                recv_sem=a2a_recv.at[which],
-                device_id=plane_device(target),
+                src_ref=send_r.at[target_group * n_group + to],
+                dst_ref=r_slot,
+                send_sem=a2a_send.at[0],
+                recv_sem=a2a_recv.at[(n_parts - part) % n_parts],
+                device_id={
+                    "rows": z * n_rs + target_group * CORES + lax.div(to, n_q),
+                    "chan": lax.rem(to, n_q),
+                },
                 device_id_type=MESH,
             ).start()
 
-        pltpu.make_async_copy(src.at[me], dst, a2a_recv.at[which]).start()
-
-    exchange(send_r, r_all.at[z, q, rs], 0)
+    @pl.when(core == 0)
+    def _():
+        pl.semaphore_wait(barrier, n_plane - n_group - 1 + 2 * CORES)
+        tell(near_sem)
+
+    @pl.when(core == 1)
+    def _():
+        pl.semaphore_wait(near_sem, 1)
+
+    pltpu.make_async_copy(send_r.at[me], r_slot, a2a_recv.at[0]).start()
+    for part in near_first[-2::-1]:
+        send_group(part)
+
+    @pl.when(core == 1)
+    def _():
+        pl.semaphore_wait(barrier, n_group + 1)
+        tell(far_sem)
+
+    @pl.when(core == 0)
+    def _():
+        pl.semaphore_wait(far_sem, 1)
+
+    send_group(opposite)
+
     project(0, send_l)
-    exchange(send_l, l_in.at[q, rs], 1)
 
     gate[...] = jax.nn.sigmoid(
         jnp.dot(normed, w_in_ref[:, 4 * width :], preferred_element_type=jnp.float32)
     )
 
     far = n_z // 2
-    n_chunks = 4
-    q_chunk = n_q // n_chunks
-    depth = q_chunk * 2 * n_k
     rows = n_rs * n_i
 
     def origin(direction, step):
         return lax.rem(z + (n_z - step if direction == 0 else step), n_z)
 
     def ring_copy(direction, step, chunk, block):
-        ref = r_all.at[block, pl.ds(chunk * q_chunk, q_chunk)]
+        ref = r_all.at[block, lax.rem(group + chunk, n_parts)]
         return pltpu.make_async_remote_copy(
             src_ref=ref,
             dst_ref=ref,
@@ -144,8 +194,8 @@
 
     def carried(direction, step):
         if step + 1 < far:
-            return range(n_chunks)
-        return range(0, n_chunks // 2) if direction == 0 else range(n_chunks // 2, n_chunks)
+            return near_first
+        return near_first[direction::2]
 
     started = []
 
@@ -158,14 +208,6 @@
     def arrive(direction, step, chunk):
         ring_copy(direction, step - 1, chunk, origin(direction, step)).wait_recv()
         forward(direction, step, chunk)
-
-    def product(block, chunk):
-        right = jnp.concatenate(
-            [r_all[block, chunk * q_chunk + k].reshape(rows, 2 * n_k) for k in range(q_chunk)], axis=1
-        )
-        return lax.dot_general(
-            l_mat[:, chunk * depth : (chunk + 1) * depth], right, NT, preferred_element_type=jnp.float32
-        )
 
     def emit(prod, block, slot):
         joined = jnp.concatenate([prod[:rows], prod[rows:]], axis=1).astype(jnp.bfloat16)
@@ -195,24 +237,33 @@
 
     def multiply(direction, step):
         block = origin(direction, step)
-        total = product(block, 0)
-        for chunk in range(1, n_chunks):
-            total = total + product(block, chunk)
-        emit(total, block, 2 * step - direction)
-
-    wait_bytes(r_all.at[z], a2a_recv.at[0])
-    for chunk in range(n_chunks):
+        right = jnp.concatenate(
+            [r_all[block, :, :, k].reshape(rows, 2 * n_k) for k in range(n_q)], axis=1
+        )
+        total = lax.dot_general(l_mat[...], right, NT, preferred_element_type=jnp.float32)
+        emit(total, block, max(2 * step - direction, 0))
+
+    for chunk in near_first:
+        wait_bytes(r_all.at[z, lax.rem(group + chunk, n_parts)], a2a_recv.at[chunk])
         for direction in (0, 1):
             forward(direction, 0, chunk)
+        if chunk == near_first[0]:
+            pltpu.make_async_copy(send_l.at[me], l_in.at[q, rs], a2a_recv.at[n_parts]).start()
+
+            @pl.loop(0, n_plane - 1)
+            def _(step):
+                away = lax.div(step + 1, 2) * (2 * lax.rem(step, 2) - 1)
+                target = lax.rem(me + n_plane // 2 + n_plane + away, n_plane)
+                send(send_l, target, l_in.at[q, rs], a2a_send.at[1], a2a_recv.at[n_parts])
 
     for step in range(1, far):
-        for chunk in range(n_chunks):
+        for at, chunk in enumerate(near_first):
             for direction in (0, 1):
                 arrive(direction, step, chunk)
-            if step > 1 and chunk in (0, n_chunks // 2):
-                multiply(0 if chunk == 0 else 1, step - 1)
+            if step > 1 and at % 2 == 0:
+                multiply(at // 2, step - 1)
         if step == 1:
-            wait_bytes(l_in, a2a_recv.at[1])
+            wait_bytes(l_in, a2a_recv.at[n_parts])
             low = lax.broadcasted_iota(jnp.int32, (rows, 2 * n_k), 1) < n_k
             for k in range(n_q):
                 block = l_in[k].reshape(rows, 2 * n_k).astype(jnp.float32)
@@ -222,18 +273,12 @@
                 l_mat[:, k * 2 * n_k : (k + 1) * 2 * n_k] = both.astype(jnp.bfloat16)
             multiply(0, 0)
 
-    last = origin(0, far)
-    total = None
-    pairs = zip(carried(0, far - 1), carried(1, far - 1), strict=True)
-    for at, chunks in enumerate(pairs):
+    for direction in (0, 1):
+        multiply(direction, far - 1)
+    for pair in zip(carried(0, far - 1), carried(1, far - 1), strict=True):
         for direction in (0, 1):
-            arrive(direction, far, chunks[direction])
-            part = product(last, chunks[direction])
-            total = part if total is None else total + part
-        if at == 0:
-            multiply(0, far - 1)
-            multiply(1, far - 1)
-    emit(total, last, 2 * far - 1)
+            arrive(direction, far, pair[direction])
+    multiply(1, far)
 
     loads[3].wait()
     w_halves = jnp.concatenate([w_out_ref[:half], w_out_ref[half:]], axis=1)
@@ -291,16 +336,18 @@
                 pltpu.VMEM((n_plane, *tile), jnp.bfloat16),
                 pltpu.VMEM((n_plane, *tile), jnp.bfloat16),
                 pltpu.VMEM((n_q, n_rs, *tile), jnp.bfloat16),
-                pltpu.VMEM((n_z, n_q, n_rs, *tile), jnp.bfloat16),
+                pltpu.VMEM((n_z, n_rs // CORES, CORES, n_q, *tile), jnp.bfloat16),
                 pltpu.VMEM((2 * n_rs * n_i, n_q * 2 * n_k), jnp.bfloat16),
                 pltpu.VMEM((n_z, n_rs, *tile), jnp.bfloat16),
                 pltpu.VMEM((n_plane, *tile), jnp.bfloat16),
                 pltpu.VMEM((n_i * n_k, width), jnp.float32),
                 pltpu.SemaphoreType.DMA((2,)),
+                pltpu.SemaphoreType.DMA((n_rs // CORES + 1,)),
+                pltpu.SemaphoreType.DMA((2, n_z // 2, n_rs // CORES)),
+                pltpu.SemaphoreType.DMA((2, n_z // 2, n_rs // CORES)),
                 pltpu.SemaphoreType.DMA((2,)),
-                pltpu.SemaphoreType.DMA((2, n_z // 2, 4)),
-                pltpu.SemaphoreType.DMA((2, n_z // 2, 4)),
-                pltpu.SemaphoreType.DMA((2,)),
+                pltpu.SemaphoreType.REGULAR,
+                pltpu.SemaphoreType.REGULAR,
             ],
             compiler_params=pltpu.CompilerParams(
                 collective_id=0, has_side_effects=True, vmem_limit_bytes=16 * 2**20

time: 46.7 us -> 44.1 us (0.944)
  Pallas kernels: 45.9 us -> 43.3 us
    pallas_call x1, Pallas kernels: 45.9 us -> 43.3 us  [on_device(): pl.pallas_call(functools.partial(kernel, n_z, n_rs, n_q), out_shape=jax.S...]
where the time goes in v3:
time: 44.1 us; the launch traced here: 44 us
  Pallas kernels  43.3 us (98%)
  local copies, waits for them, and re-layouts  0.66 us (1%)
    pallas_call x1, Pallas kernels, on_device(): pl.pallas_call(functools.partial(kernel, n_z, n_rs, n_q), out_shape=jax.S...  43.3 us

profile of v3, /device:TPU:9, one launch (start us, length us, event | category | flops | bytes accessed | tf_op | source)
XLA Modules:
  0.0 44.0 jit_solution(12347641309361485294)
XLA Ops:
  0.0 43.3 %shard_map.46 = bf16[8,64,128]{2,1,0:T(8,128)(2,1)S(1)} custom-call(s32[4,4]{1,0:T(4,128)} %mask_hbm.1, bf16[8,64,128]{2,1,0:T(8,128)(2,1)} %pair_hbm.1, bf16[128,640]{1,0:T(8,128)(2,1)} %w_in_hbm.1, bf16[128,128]{1,0:T(8,128)(2,1)} %w_out_hbm.1), custom_call_target="tpu_custom_call" | custom-call | tf_op jit(solution)/shard_map/pallas_call | solution.py:324
  43.3 0.7 %copy.6 = bf16[8,64,128]{2,1,0:T(8,128)(2,1)} copy(bf16[8,64,128]{2,1,0:T(8,128)(2,1)S(1)} %shard_map.46) | data formatting | bytes 262144

commit v4 on v3

--- a/solution.py
+++ b/solution.py
@@ -11,6 +11,10 @@
 EPS = 1e-05
 CORES = 2
 UNROLL = 4
+UNROLL_L = 7
+SEND_LEFT = 1
+LEFT_STEP = 1
+POPS = 2
 MESH = pl.DeviceIdType.MESH
 NT = (((1,), (1,)), ((), ()))
 
@@ -155,19 +159,29 @@
         pl.semaphore_wait(near_sem, 1)
 
     pltpu.make_async_copy(send_r.at[me], r_slot, a2a_recv.at[0]).start()
+    def hear_far():
+        @pl.when(core == 1)
+        def _():
+            pl.semaphore_wait(barrier, n_group + 1)
+            tell(far_sem)
+
+        @pl.when(core == 0)
+        def _():
+            pl.semaphore_wait(far_sem, 1)
+
+    @pl.when(group == opposite)
+    def _():
+        hear_far()
+        send_group(opposite)
+
     for part in near_first[-2::-1]:
         send_group(part)
 
-    @pl.when(core == 1)
+    @pl.when(group != opposite)
     def _():
-        pl.semaphore_wait(barrier, n_group + 1)
-        tell(far_sem)
-
-    @pl.when(core == 0)
-    def _():
-        pl.semaphore_wait(far_sem, 1)
-
-    send_group(opposite)
+        hear_far()
+        send_group(opposite)
+
 
     project(0, send_l)
 
@@ -213,7 +227,7 @@
         joined = jnp.concatenate([prod[:rows], prod[rows:]], axis=1).astype(jnp.bfloat16)
         out_send[slot] = joined.reshape(n_rs, n_i, 2 * n_k)
 
-        @pl.loop(0, n_rs)
+        @pl.loop(0, n_rs, unroll=True)
         def _(step):
             target = lax.rem(rs + n_rs // 2 + step, n_rs)
             local = jnp.logical_and(target == rs, block == q)
@@ -243,38 +257,45 @@
         total = lax.dot_general(l_mat[...], right, NT, preferred_element_type=jnp.float32)
         emit(total, block, max(2 * step - direction, 0))
 
-    for chunk in near_first:
-        wait_bytes(r_all.at[z, lax.rem(group + chunk, n_parts)], a2a_recv.at[chunk])
+    def send_left():
+        pltpu.make_async_copy(send_l.at[me], l_in.at[q, rs], a2a_recv.at[n_parts]).start()
+
+        @pl.loop(0, n_plane - 1, unroll=UNROLL_L)
+        def _(step):
+            away = lax.div(step + 1, 2) * (2 * lax.rem(step, 2) - 1)
+            target = lax.rem(me + n_plane // 2 + n_plane + away, n_plane)
+            send(send_l, target, l_in.at[q, rs], a2a_send.at[1], a2a_recv.at[n_parts])
+
+    def spread_left():
+        wait_bytes(l_in, a2a_recv.at[n_parts])
+        low = lax.broadcasted_iota(jnp.int32, (rows, 2 * n_k), 1) < n_k
+        for k in range(n_q):
+            block = l_in[k].reshape(rows, 2 * n_k).astype(jnp.float32)
+            both = jnp.concatenate([jnp.where(low, block, 0.0), jnp.where(low, 0.0, block)], axis=0)
+            l_mat[:, k * 2 * n_k : (k + 1) * 2 * n_k] = both.astype(jnp.bfloat16)
+        multiply(0, 0)
+
+    for at, part in enumerate(near_first):
+        wait_bytes(r_all.at[z, lax.rem(group + part, n_parts)], a2a_recv.at[part])
+        if at + 1 == SEND_LEFT:
+            pl.when(core == 1)(send_left)
         for direction in (0, 1):
-            forward(direction, 0, chunk)
-        if chunk == near_first[0]:
-            pltpu.make_async_copy(send_l.at[me], l_in.at[q, rs], a2a_recv.at[n_parts]).start()
-
-            @pl.loop(0, n_plane - 1)
-            def _(step):
-                away = lax.div(step + 1, 2) * (2 * lax.rem(step, 2) - 1)
-                target = lax.rem(me + n_plane // 2 + n_plane + away, n_plane)
-                send(send_l, target, l_in.at[q, rs], a2a_send.at[1], a2a_recv.at[n_parts])
-
+            forward(direction, 0, part)
+        if at + 1 == SEND_LEFT:
+            pl.when(core == 0)(send_left)
+
+    work = [spread_left]
     for step in range(1, far):
-        for at, chunk in enumerate(near_first):
+        for at, part in enumerate(near_first):
             for direction in (0, 1):
-                arrive(direction, step, chunk)
-            if step > 1 and at % 2 == 0:
-                multiply(at // 2, step - 1)
-        if step == 1:
-            wait_bytes(l_in, a2a_recv.at[n_parts])
-            low = lax.broadcasted_iota(jnp.int32, (rows, 2 * n_k), 1) < n_k
-            for k in range(n_q):
-                block = l_in[k].reshape(rows, 2 * n_k).astype(jnp.float32)
-                both = jnp.concatenate(
-                    [jnp.where(low, block, 0.0), jnp.where(low, 0.0, block)], axis=0
-                )
-                l_mat[:, k * 2 * n_k : (k + 1) * 2 * n_k] = both.astype(jnp.bfloat16)
-            multiply(0, 0)
-
-    for direction in (0, 1):
-        multiply(direction, far - 1)
+                arrive(direction, step, part)
+            if step > LEFT_STEP and work and at % (n_parts // POPS) == 0:
+                work.pop(0)()
+        work += [functools.partial(multiply, direction, step) for direction in (0, 1)]
+        if step == LEFT_STEP:
+            work.pop(0)()
+    for item in work:
+        item()
     for pair in zip(carried(0, far - 1), carried(1, far - 1), strict=True):
         for direction in (0, 1):
             arrive(direction, far, pair[direction])
@@ -292,7 +313,7 @@
         centered = values - mean
         square = jnp.sum(centered * centered, axis=0, keepdims=True)
         var = (square + pltpu.roll(square, n_k, 1)) * (1.0 / width)
-        turned.append((centered / jnp.sqrt(var + EPS)).T.astype(jnp.bfloat16))
+        turned.append((centered * (1.0 / jnp.sqrt(var + EPS))).T.astype(jnp.bfloat16))
     mixed = jnp.dot(
         jnp.concatenate(turned, axis=0), w_halves, preferred_element_type=jnp.float32
     )

time: 44.1 us -> 44 us (level)
  no operation moved by 1% of the time
where the time goes in v4:
time: 44 us; the launch traced here: 43.9 us
  Pallas kernels  43.2 us (98%)
  local copies, waits for them, and re-layouts  0.66 us (2%)
    pallas_call x1, Pallas kernels, on_device(): pl.pallas_call(functools.partial(kernel, n_z, n_rs, n_q), out_shape=jax.S...  43.2 us

profile of v4, /device:TPU:9, one launch (start us, length us, event | category | flops | bytes accessed | tf_op | source)
XLA Modules:
  0.0 43.9 jit_solution(2297968604173966710)
XLA Ops:
  0.0 43.2 %shard_map.46 = bf16[8,64,128]{2,1,0:T(8,128)(2,1)S(1)} custom-call(s32[4,4]{1,0:T(4,128)} %mask_hbm.1, bf16[8,64,128]{2,1,0:T(8,128)(2,1)} %pair_hbm.1, bf16[128,640]{1,0:T(8,128)(2,1)} %w_in_hbm.1, bf16[128,128]{1,0:T(8,128)(2,1)} %w_out_hbm.1), custom_call_target="tpu_custom_call" | custom-call | tf_op jit(solution)/shard_map/pallas_call | solution.py:345
  43.2 0.7 %copy.6 = bf16[8,64,128]{2,1,0:T(8,128)(2,1)} copy(bf16[8,64,128]{2,1,0:T(8,128)(2,1)S(1)} %shard_map.46) | data formatting | bytes 262144

commit v5 on v3

--- a/solution.py
+++ b/solution.py
@@ -10,6 +10,7 @@
 BLOCK = 128
 EPS = 1e-05
 CORES = 2
+PIECES = 4
 UNROLL = 4
 MESH = pl.DeviceIdType.MESH
 NT = (((1,), (1,)), ((), ()))
@@ -32,7 +33,16 @@
             [(pair_hbm, pair_ref), (w_in_hbm, w_in_ref), (mask_hbm, mask_ref), (w_out_hbm, w_out_ref)]
         )
     ]
-    for load in loads:
+    quarter = pair_hbm.shape[0] // PIECES
+    pieces = [
+        pltpu.make_async_copy(
+            pair_hbm.at[pl.ds(at * quarter, quarter)],
+            pair_ref.at[pl.ds(at * quarter, quarter)],
+            load_sems.at[4 + at],
+        )
+        for at in range(PIECES)
+    ]
+    for load in pieces + loads[1:]:
         load.start()
     n_i, n_k, width = pair_ref.shape
     half = width // 2
@@ -71,7 +81,8 @@
     for neighbour in (up, down):
         hello({"rows": neighbour["rows"] - core, "chan": q})
 
-    loads[0].wait()
+    for piece in pieces:
+        piece.wait()
     cells = pair_ref[...].astype(jnp.float32).reshape(n_i * n_k, width)
     mean = jnp.mean(cells, axis=-1, keepdims=True)
     centered = cells - mean
@@ -213,7 +224,7 @@
         joined = jnp.concatenate([prod[:rows], prod[rows:]], axis=1).astype(jnp.bfloat16)
         out_send[slot] = joined.reshape(n_rs, n_i, 2 * n_k)
 
-        @pl.loop(0, n_rs)
+        @pl.loop(0, n_rs, unroll=True)
         def _(step):
             target = lax.rem(rs + n_rs // 2 + step, n_rs)
             local = jnp.logical_and(target == rs, block == q)
@@ -331,7 +342,7 @@
                 pltpu.VMEM(pair.shape, pair.dtype),
                 pltpu.VMEM(w_in.shape, w_in.dtype),
                 pltpu.VMEM(w_out.shape, w_out.dtype),
-                pltpu.SemaphoreType.DMA((4,)),
+                pltpu.SemaphoreType.DMA((4 + PIECES,)),
                 pltpu.VMEM((n_plane * n_i, 2 * n_k), jnp.float32),
                 pltpu.VMEM((n_plane, *tile), jnp.bfloat16),
                 pltpu.VMEM((n_plane, *tile), jnp.bfloat16),

time: 44.1 us -> 44.1 us (level)
  no operation moved by 1% of the time
where the time goes in v5:
time: 44.1 us; the launch traced here: 44 us
  Pallas kernels  43.3 us (98%)
  local copies, waits for them, and re-layouts  0.66 us (1%)
    pallas_call x1, Pallas kernels, on_device(): pl.pallas_call(functools.partial(kernel, n_z, n_rs, n_q), out_shape=jax.S...  43.3 us

profile of v5, /device:TPU:9, one launch (start us, length us, event | category | flops | bytes accessed | tf_op | source)
XLA Modules:
  0.0 44.0 jit_solution(4561995597675125615)
XLA Ops:
  0.0 43.3 %shard_map.46 = bf16[8,64,128]{2,1,0:T(8,128)(2,1)S(1)} custom-call(s32[4,4]{1,0:T(4,128)} %mask_hbm.1, bf16[8,64,128]{2,1,0:T(8,128)(2,1)} %pair_hbm.1, bf16[128,640]{1,0:T(8,128)(2,1)} %w_in_hbm.1, bf16[128,128]{1,0:T(8,128)(2,1)} %w_out_hbm.1), custom_call_target="tpu_custom_call" | custom-call | tf_op jit(solution)/shard_map/pallas_call | solution.py:335
  43.3 0.7 %copy.6 = bf16[8,64,128]{2,1,0:T(8,128)(2,1)} copy(bf16[8,64,128]{2,1,0:T(8,128)(2,1)S(1)} %shard_map.46) | data formatting | bytes 262144
